TPU v7x, 32 devices: a whole 2x2x4 slice. The times are simulated.
32 devices in a mesh: section: 4 (over z), expert: 8 (over y, x, core).
Axes of the slice: x: 2, y: 2, z: 4, core: 2. Of those that a mesh axis runs over, the one named last changes fastest.
Arguments:
- tokens: bfloat16 [96, 3584], P('expert', 'section'), may hold values from -6 to 6
- scales: float32 [96, 28], P('expert'), may hold values from 0.25 to 4
- expert_ids: int32 [96, 8], P('expert'), may hold values from 0 to 63, all different within a row; in each aligned block of 12 rows (0 to 11, 12 to 23, ...) at most 2 rows name the same one
- gate_fixed: int32 [96, 8], P('expert'), may hold values from 1 to 65535
- w_gate: bfloat16 [64, 3584, 2048], P('expert', None, 'section'), may hold values from -0.09375 to 0.09375
- w_up: bfloat16 [64, 3584, 2048], P('expert', None, 'section'), may hold values from -0.09375 to 0.09375
- w_down: bfloat16 [64, 2048, 3584], P('expert', 'section'), may hold values from -0.125 to 0.125
Outputs:
- mixed: bfloat16 [96, 3584], P('expert', 'section')
Inputs may be any that keep to these rules, and one draw needn't show every extreme that they name: `expert_ids`: each row names 8 different experts. Among the 12 rows of one device (aligned blocks of 12 rows) no expert is named more than 2 times; in some block some expert is named exactly 2 times.
All inputs are finite; a program needn't handle non-finite values.
Results may differ from a plain program's by a relative error of at most 0.018.
Values may be sent and summed in bfloat16 or wider, within the bound.
A program may use at most 192 MiB of HBM per device.

v0:
```python
import jax
import jax.numpy as jnp
from jax import lax
from jax.sharding import PartitionSpec as P


def shards(tokens, scales, expert_ids, gate_fixed, w_gate, w_up, w_down):
    n_expert = lax.axis_size("expert")
    tok_rows, local_width = tokens.shape
    block_count = scales.shape[1]
    top_count = expert_ids.shape[1]
    exp_local = w_gate.shape[0]
    experts_all = exp_local * n_expert
    capacity = tok_rows // 6
    column_ids = lax.axis_index("section") * local_width + jnp.arange(local_width, dtype=jnp.int32)
    block_table = (
        jnp.arange(block_count, dtype=jnp.int32)[:, None] == (column_ids // 128)[None, :]
    ).astype(jnp.float32)
    scale_cols = jnp.dot(scales, block_table, precision=lax.Precision.HIGHEST)
    dequant = (tokens.astype(jnp.float32) * scale_cols).astype(jnp.bfloat16)
    flat_ids = expert_ids.reshape(-1)
    onehot = (flat_ids[:, None] == jnp.arange(experts_all, dtype=jnp.int32)[None, :]).astype(
        jnp.int32
    )
    earlier = jnp.cumsum(onehot, axis=0) - onehot
    position = jnp.sum(earlier * onehot, axis=1)
    slot_flat = (flat_ids * capacity + position).reshape(tok_rows, top_count)
    chooser = jnp.any(
        jnp.arange(experts_all * capacity, dtype=jnp.int32)[:, None, None] == slot_flat[None, :, :],
        axis=2,
    ).astype(jnp.bfloat16)
    outgoing = jnp.dot(chooser, dequant, preferred_element_type=jnp.float32).astype(jnp.bfloat16)
    outgoing = outgoing.reshape(n_expert, exp_local, capacity, local_width)
    whole = lax.all_gather(
        lax.all_to_all(outgoing, "expert", split_axis=0, concat_axis=0, tiled=True),
        "section",
        axis=3,
        tiled=True,
    )
    gate_part = jnp.einsum("seld,edf->self", whole, w_gate, preferred_element_type=jnp.float32)
    up_part = jnp.einsum("seld,edf->self", whole, w_up, preferred_element_type=jnp.float32)
    hidden = (jax.nn.silu(gate_part) * up_part).astype(jnp.bfloat16)
    partial_rows = jnp.einsum(
        "self,efd->seld", hidden, w_down, preferred_element_type=jnp.float32
    ).astype(jnp.bfloat16)
    weights = gate_fixed.astype(jnp.float32) * (1.0 / 65536.0)
    summed = lax.psum_scatter(
        partial_rows.astype(jnp.float32).astype(jnp.bfloat16),
        "section",
        scatter_dimension=3,
        tiled=True,
    ).astype(jnp.float32)
    returned = lax.all_to_all(
        summed.astype(jnp.bfloat16), "expert", split_axis=0, concat_axis=0, tiled=True
    ).astype(summed.dtype)
    returned = returned.reshape(experts_all * capacity, returned.shape[3])
    picked = returned[slot_flat]
    return jnp.sum(picked * weights[:, :, None], axis=1).astype(jnp.bfloat16)


def solution(mesh):
    placed = (
        P("expert", "section"),
        P("expert", None),
        P("expert", None),
        P("expert", None),
        P("expert", None, "section"),
        P("expert", None, "section"),
        P("expert", "section", None),
    )
    return jax.shard_map(
        shards, mesh=mesh, in_specs=placed, out_specs=P("expert", "section"), check_vma=False
    )
```

profile of v0, /device:TPU:0, one launch (start us, length us, event | category | flops | bytes accessed | tf_op | source)
XLA Modules:
  0.0 199.2 jit_solution(2657194242331982782)
XLA Ops:
  6.5 0.0 copy-start
  6.5 0.0 reduce-scatter.4.cloned.1.call-start
  6.5 0.8 copy.22
  7.3 0.1 eq.42
  7.4 0.1 fusion.36
  7.5 0.1 reduce_window_sum.11
  7.6 0.2 select_reduce_fusion
  7.8 0.1 reduce_sum.21
  7.9 0.1 fusion.37
  8.0 0.0 copy-done
  8.0 0.9 fusion.27
  9.0 0.3 convolution_convert_fusion
  9.3 0.1 reshape.39
  9.4 11.5 %all_to_all.10 = bf16[8,8,2,896]{3,2,1,0:T(2,128)(2,1)S(1)} all-to-all(bf16[8,8,2,896]{3,2,1,0:T(2,128)(2,1)S(1)} %reshape.39), channel_id=1, replica_groups=mesh['section'=4,'expert'=8] {'expert'}, dimensions={0} | all-to-all | bytes 458752 | tf_op jit(solution)/shard_map/all_to_all | solution.py:35
  20.9 21.3 %all_gather.3 = bf16[8,8,2,3584]{3,0,2,1:T(8,128)(2,1)S(1)} all-gather(bf16[8,8,2,896]{3,0,2,1:T(8,128)(2,1)S(1)} %copy.24), channel_id=1, replica_groups=mesh['section'=4,'expert'=8] {'section'}, dimensions={3}, use_global_device_ids=true | all-gather | bytes 1146880 | tf_op jit(solution)/shard_map/all_gather | solution.py:34
  42.3 11.3 %fusion.12 = f32[8,8,2,512]{3,0,2,1:T(8,128)S(1)} fusion(bf16[8,8,2,3584]{3,0,2,1:T(8,128)(2,1)S(1)} %all_gather.3, bf16[8,3584,512]{2,1,0:T(8,128)(2,1)} %param.11), kind=kOutput, calls=%fused_computation.10 | convolution fusion | flops 469762048 | bytes 30539776 | tf_op jit(solution)/shard_map/seld,edf->self/dot_general | solution.py:40
  53.6 0.0 copy-start.1
  53.6 20.1 %fusion.9 = bf16[8,8,2,3584]{3,0,2,1:T(8,128)(2,1)S(1)} fusion(bf16[8,512,3584]{2,1,0:T(8,128)(2,1)} %param.13, bf16[8,8,2,3584]{3,0,2,1:T(8,128)(2,1)S(1)} %all_gather.3, bf16[8,3584,512]{2,1,0:T(8,128)(2,1)} %param.12, f32[8,8,2,512]{3,0,2,1:T(8,128)S(1)} %fusion.12), kind=kOutput, calls=%fused_computation.8 | convolution fusion | flops 940376064 | bytes 60817408 | tf_op jit(solution)/shard_map/self,efd->seld/dot_general | solution.py:43
  73.7 0.0 copy-start.2
  73.7 24.1 %copy.30 = bf16[8,8,2,3584]{0,2,1,3:T(2,128)(2,1)} copy(bf16[8,8,2,3584]{3,0,2,1:T(8,128)(2,1)S(1)} %fusion.9) | data formatting | bytes 1835008
  97.8 38.3 %reshape.57 = bf16[3584,128]{1,0:T(8,128)(2,1)} reshape(bf16[3584,8,2,8]{3,2,1,0:T(2,128)(2,1)} %bitcast.59) | data formatting | bytes 1835008
  136.1 0.0 reduce-scatter.4.cloned.1.call-update
  136.1 23.0 %reduce-scatter.4.cloned.1.call-done = bf16[896,128]{1,0:T(8,128)(2,1)} async-done(((bf16[3584,128]{1,0:T(8,128)(2,1)}), bf16[896,128]{1,0:T(8,128)(2,1)}) %reduce-scatter.4.cloned.1.call-update) | async-done | bytes 229392
  159.1 12.0 %reshape.58 = bf16[896,8,2,8]{3,2,1,0:T(2,128)(2,1)} reshape(bf16[896,128]{1,0:T(8,128)(2,1)} %reduce-scatter.4.cloned.1.call-done) | data formatting | bytes 458752
  171.1 9.4 %copy.25 = bf16[8,8,2,896]{3,2,1,0:T(2,128)(2,1)} copy(bf16[8,8,2,896]{0,2,1,3:T(2,128)(2,1)} %bitcast.60) | data formatting | bytes 458752 | tf_op jit(solution)/shard_map/reduce_scatter | solution.py:47
  180.5 3.7 %all-to-all-start.1 = ((bf16[8,8,2,896]{3,2,1,0:T(2,128)(2,1)}), bf16[8,8,2,896]{3,2,1,0:T(2,128)(2,1)S(1)}, u32[]{:S(2)}, u32[]{:S(2)}) async-start(bf16[8,8,2,896]{3,2,1,0:T(2,128)(2,1)} %copy.25), calls=%async_computation.1 | async-start | bytes 458752 | tf_op jit(solution)/shard_map/all_to_all | solution.py:53
  184.2 0.0 copy-done.2
  184.2 0.1 reshape.46
  184.3 0.1 copy.26
  184.4 6.4 %all-to-all-done.1 = bf16[8,8,2,896]{3,2,1,0:T(2,128)(2,1)S(1)} async-done(((bf16[8,8,2,896]{3,2,1,0:T(2,128)(2,1)}), bf16[8,8,2,896]{3,2,1,0:T(2,128)(2,1)S(1)}, u32[]{:S(2)}, u32[]{:S(2)}) %all-to-all-start.1) | async-done | bytes 229408 | tf_op jit(solution)/shard_map/all_to_all | solution.py:53
  190.7 0.1 reshape.43
  190.8 0.8 gather_fusion
  191.5 0.8 fusion.28
  192.3 0.0 copy-done.1
  (5 shorter events, 0.1 us)
Async XLA Ops:
  6.5 1.5 copy-start
  6.5 152.5 %reduce-scatter.4.cloned.1.call-start = ((), (), s32[]{:S(2)}) async-start(), calls=%async_computation.3 | async-start | bytes 1146880
  53.6 138.7 %copy-start.1 = (f32[12,28]{1,0:T(8,128)S(1)}, f32[12,28]{1,0:T(8,128)}, u32[]{:S(2)}) copy-start(f32[12,28]{1,0:T(8,128)} %param.8) | copy-start | bytes 4036
  73.7 110.5 %copy-start.2 = (s32[12,8]{0,1:T(8,128)S(1)}, s32[12,8]{0,1:T(8,128)}, u32[]{:S(2)}) copy-start(s32[12,8]{0,1:T(8,128)} %param.10) | copy-start | bytes 1156
  180.5 10.2 %all-to-all-start.1 = ((bf16[8,8,2,896]{3,2,1,0:T(2,128)(2,1)}), bf16[8,8,2,896]{3,2,1,0:T(2,128)(2,1)S(1)}, u32[]{:S(2)}, u32[]{:S(2)}) async-start(bf16[8,8,2,896]{3,2,1,0:T(2,128)(2,1)} %copy.25), calls=%async_computation.1 | async-start | bytes 458752 | tf_op jit(solution)/shard_map/all_to_all | solution.py:53
Sparse Core Ops, SparseCore 0:
  136.2 22.8 reduce-scatter.3
where the time goes:
time: 200 us; the launch traced here: 199 us
  local copies, waits for them, and re-layouts  85.9 us (43%)
  blocking collectives  32.9 us (16%)
  matrix products  32.6 us (16%)
  waiting for transfers between devices  29.3 us (15%)
  between operations  13.5 us (7%)
  starting transfers between devices  3.68 us (2%)
    unnamed x10, local copies, waits for them, and re-layouts  75.2 us
    unnamed x2, waiting for transfers between devices  23 us
    all_gather x1, blocking collectives, shards(): lax.all_gather(lax.all_to_all(outgoing, 'expert', split_axis=0, concat_ax...  21.3 us
    dot_general x1, matrix products, shards(): jnp.einsum('self,efd->seld', hidden, w_down, preferred_element_type=jnp.f...  20.1 us
    all_to_all x1, blocking collectives, shards(): lax.all_to_all(outgoing, 'expert', split_axis=0, concat_axis=0, tiled=True)  11.5 us
    dot_general x1, matrix products, shards(): jnp.einsum('seld,edf->self', whole, w_gate, preferred_element_type=jnp.fl...  11.3 us
    reduce_scatter x1, local copies, waits for them, and re-layouts, shards(): lax.psum_scatter(partial_rows.astype(jnp.float32).astype(jnp.bfloat16), '...  9.41 us
    all_to_all x1, waiting for transfers between devices, shards(): lax.all_to_all(summed.astype(jnp.bfloat16), 'expert', split_axis=0, conca...  6.36 us
  transfers between devices with their start and end apart: 2, of which 2 were waited for; matrix products, arithmetic and copies ran while one was open for 0% of the time, Pallas kernels for 0%

commit v1 on v0

--- a/solution.py
+++ b/solution.py
@@ -1,6 +1,10 @@
+import functools
+
 import jax
 import jax.numpy as jnp
 from jax import lax
+from jax.experimental import pallas as pl
+from jax.experimental.pallas import tpu as pltpu
 from jax.sharding import PartitionSpec as P
 
 
@@ -58,6 +62,305 @@
     return jnp.sum(picked * weights[:, :, None], axis=1).astype(jnp.bfloat16)
 
 
+MESH = pl.DeviceIdType.MESH
+VMEM_BYTES = 67043328
+HALVES = 2
+
+
+def layer_kernel(
+    n_sec, n_exp, depth,
+    tok_ref, sc_ref, id_ref, gf_ref, wg_ref, wu_ref, wd_ref, o_ref,
+    gbuf, ubuf, dbuf, xg, x2, gates, gates2, hid, acc, part, landed, sect, sect_in,
+    w_sem, d_sem, z_send, z_recv, p_send, p_recv, c_send, c_recv, g_send, g_recv,
+    a_send, a_recv, b_send, b_recv,
+):
+    sec, me = lax.axis_index("section"), lax.axis_index("expert")
+    rows, width = tok_ref.shape
+    exp_local, features, hidden = wg_ref.shape
+    pad = x2.shape[0] // n_exp
+    per_half = exp_local // HALVES
+    sib = me + 1 - 2 * lax.rem(me, 2)
+    peers = [lax.rem(me + d, n_exp) for d in range(n_exp)]
+    senders = [lax.rem(me + n_exp - d, n_exp) for d in range(n_exp)]
+
+    def gate_copy(e):
+        slot = lax.rem(e, depth)
+        return pltpu.make_async_copy(wg_ref.at[e], gbuf.at[slot], w_sem.at[slot, 0])
+
+    def up_copy(e):
+        slot = lax.rem(e, depth)
+        return pltpu.make_async_copy(wu_ref.at[e], ubuf.at[slot], w_sem.at[slot, 1])
+
+    def down_copy(half, c):
+        column = pl.multiple_of(lax.rem(sec + 1 + c, n_sec) * width, 128)
+        return pltpu.make_async_copy(
+            wd_ref.at[pl.ds(half * per_half, per_half), :, pl.ds(column, width)],
+            dbuf.at[c],
+            d_sem.at[c],
+        )
+
+    for e in range(per_half):
+        gate_copy(e).start()
+        up_copy(e).start()
+    for c in range(n_sec):
+        down_copy(0, c).start()
+    for e in range(per_half, depth):
+        gate_copy(e).start()
+        up_copy(e).start()
+
+    barrier = pltpu.get_barrier_semaphore()
+    for d in range(1, n_sec):
+        pl.semaphore_signal(
+            barrier, inc=1, device_id=(lax.rem(sec + d, n_sec), me), device_id_type=MESH
+        )
+    for d in range(1, n_exp):
+        pl.semaphore_signal(barrier, inc=1, device_id=(sec, peers[d]), device_id_type=MESH)
+
+    scales = sc_ref[...]
+    block_ids = lax.broadcasted_iota(jnp.int32, scales.shape, 1)
+    for j in range(width // 128):
+        block = sec * (width // 128) + j
+        scale = jnp.sum(jnp.where(block_ids == block, scales, 0.0), axis=1, keepdims=True)
+        cols = slice(j * 128, (j + 1) * 128)
+        xg[me, sec, :, cols] = (tok_ref[:, cols].astype(jnp.float32) * scale).astype(jnp.bfloat16)
+    ids = id_ref[...]
+    weights = gf_ref[...].astype(jnp.float32) * (1.0 / 65536.0)
+    expert_row = lax.broadcasted_iota(jnp.int32, gates.shape[1:], 1)
+    table = jnp.zeros(gates.shape[1:], jnp.float32)
+    for k in range(ids.shape[1]):
+        table = table + jnp.where(expert_row == ids[:, k : k + 1], weights[:, k : k + 1], 0.0)
+    gates[me] = table
+    x2[...] = jnp.zeros_like(x2)
+    gates2[...] = jnp.zeros_like(gates2)
+
+    pl.semaphore_wait(barrier, n_sec - 1 + n_exp - 1)
+
+    def z_copy(d):
+        return pltpu.make_async_remote_copy(
+            xg.at[me, sec], xg.at[me, sec], z_send.at[d], z_recv.at[d],
+            device_id=(lax.rem(sec + d, n_sec), me), device_id_type=MESH,
+        )
+
+    def z_in(d):
+        slot = xg.at[me, lax.rem(sec + n_sec - d, n_sec)]
+        return pltpu.make_async_remote_copy(
+            slot, slot, z_send.at[d], z_recv.at[d],
+            device_id=(lax.rem(sec + d, n_sec), me), device_id_type=MESH,
+        )
+
+    def move(block, send, recv, to):
+        return pltpu.make_async_remote_copy(
+            block, block, send, recv, device_id=(sec, to), device_id_type=MESH
+        )
+
+    def gate_move(block, d):
+        return move(gates.at[block], g_send.at[d], g_recv.at[d], peers[d])
+
+    chips = list(range(2, n_exp, 2))
+    for d in range(1, n_sec):
+        z_copy(d).start()
+    for d in range(1, n_exp):
+        gate_move(me, d).start()
+    for d in range(1, n_sec):
+        z_in(d).wait_recv()
+    for d in chips:
+        move(xg.at[me], p_send.at[d], p_recv.at[d], peers[d]).start()
+    move(xg.at[me], c_send.at[0], c_recv.at[0], sib).start()
+    for d in chips:
+        block = xg.at[senders[d]]
+        move(block, p_send.at[d], p_recv.at[d], peers[d]).wait_recv()
+        move(block, c_send.at[d], c_recv.at[d], sib).start()
+    for d in [0] + chips:
+        block = xg.at[lax.rem(sib + n_exp - d, n_exp)]
+        move(block, c_send.at[d], c_recv.at[d], sib).wait_recv()
+    for d in range(1, n_exp):
+        gate_move(senders[d], d).wait_recv()
+
+    for b in range(n_exp):
+        for s in range(n_sec):
+            x2[b * pad : b * pad + rows, s * width : (s + 1) * width] = xg[b, s]
+        gates2[b * pad : b * pad + rows, :] = gates[b]
+
+    def expert(e, half):
+        slot = lax.rem(e, depth)
+        gate_copy(e).wait()
+        up_copy(e).wait()
+        lanes = lax.broadcasted_iota(jnp.int32, gates2.shape, 1)
+        chosen = jnp.sum(
+            jnp.where(lanes == me * exp_local + e, gates2[...], 0.0), axis=1, keepdims=True
+        )
+        step = TILE if hidden % TILE == 0 else hidden
+        for n in range(0, hidden, step):
+            gate = jnp.dot(
+                x2[...], gbuf[slot, :, n : n + step], preferred_element_type=jnp.float32
+            )
+            up = jnp.dot(x2[...], ubuf[slot, :, n : n + step], preferred_element_type=jnp.float32)
+            value = (jax.nn.silu(gate) * up * chosen).astype(jnp.bfloat16)
+            hid[:, pl.ds(pl.multiple_of((e - half * per_half) * hidden + n, 128), step)] = value
+
+        @pl.when(e + depth < exp_local)
+        def _():
+            gate_copy(e + depth).start()
+            up_copy(e + depth).start()
+
+    def product(c):
+        down = dbuf[c].reshape(per_half * hidden, width)
+        return jnp.dot(hid[...], down, preferred_element_type=jnp.float32)
+
+    @pl.loop(0, per_half)
+    def _(e):
+        expert(e, 0)
+
+    @pl.loop(0, n_sec)
+    def _(c):
+        down_copy(0, c).wait()
+        acc[c] = product(c)
+        down_copy(1, c).start()
+
+    @pl.loop(per_half, exp_local)
+    def _(e):
+        expert(e, 1)
+
+    def a_copy(c, d):
+        return pltpu.make_async_remote_copy(
+            part.at[c, peers[d]], landed.at[c, me], a_send.at[c, d], a_recv.at[c, d],
+            device_id=(sec, peers[d]), device_id_type=MESH,
+        )
+
+    def a_in(c, d):
+        return pltpu.make_async_remote_copy(
+            part.at[c, peers[d]], landed.at[c, senders[d]], a_send.at[c, d], a_recv.at[c, d],
+            device_id=(sec, peers[d]), device_id_type=MESH,
+        )
+
+    def b_copy(c):
+        return pltpu.make_async_remote_copy(
+            sect.at[c], sect_in.at[c], b_send.at[c], b_recv.at[c],
+            device_id=(lax.rem(sec + 1 + c, n_sec), me), device_id_type=MESH,
+        )
+
+    def over_experts(c):
+        total = part[c, me].astype(jnp.float32)
+        for d in range(1, n_exp):
+            a_in(c, d).wait_recv()
+            total = total + landed[c, senders[d]].astype(jnp.float32)
+        return total
+
+    @pl.loop(0, n_sec)
+    def _(c):
+        down_copy(1, c).wait()
+        acc[c] = acc[c] + product(c)
+        for b in range(n_exp):
+            part[c, b] = acc[c, b * pad : b * pad + rows, :].astype(jnp.bfloat16)
+        for d in range(1, n_exp):
+            a_copy(c, d).start()
+
+        @pl.when(c >= 1)
+        def _():
+            sect[c - 1] = over_experts(c - 1).astype(jnp.bfloat16)
+            b_copy(c - 1).start()
+
+    total = over_experts(n_sec - 1)
+    for c in range(n_sec - 1):
+        b_copy(c).wait_recv()
+        total = total + sect_in[c].astype(jnp.float32)
+    o_ref[...] = total.astype(o_ref.dtype)
+
+    for d in range(1, n_sec):
+        z_copy(d).wait_send()
+    for d in range(1, n_exp):
+        gate_move(me, d).wait_send()
+    for d in chips:
+        move(xg.at[me], p_send.at[d], p_recv.at[d], peers[d]).wait_send()
+        move(xg.at[senders[d]], c_send.at[d], c_recv.at[d], sib).wait_send()
+    move(xg.at[me], c_send.at[0], c_recv.at[0], sib).wait_send()
+
+    @pl.loop(0, n_sec)
+    def _(c):
+        for d in range(1, n_exp):
+            a_copy(c, d).wait_send()
+
+    @pl.loop(0, n_sec - 1)
+    def _(c):
+        b_copy(c).wait_send()
+
+
+TILE = 256
+
+
+def sizes(n_sec, n_exp, tokens, w_gate, experts_all):
+    rows, width = tokens.shape
+    exp_local, features, hidden = w_gate.shape
+    pad = -(-rows // 16) * 16
+    half = exp_local // HALVES
+    scratch = [
+        ((n_exp, n_sec, rows, width), jnp.bfloat16),
+        ((n_exp * pad, features), jnp.bfloat16),
+        ((n_exp, rows, experts_all), jnp.float32),
+        ((n_exp * pad, experts_all), jnp.float32),
+        ((n_exp * pad, half * hidden), jnp.bfloat16),
+        ((n_sec, n_exp * pad, width), jnp.float32),
+        ((n_sec, n_exp, rows, width), jnp.bfloat16),
+        ((n_sec, n_exp, rows, width), jnp.bfloat16),
+        ((n_sec - 1, rows, width), jnp.bfloat16),
+        ((n_sec - 1, rows, width), jnp.bfloat16),
+    ]
+    return pad, scratch
+
+
+def fused(tokens, scales, expert_ids, gate_fixed, w_gate, w_up, w_down):
+    n_sec, n_exp = lax.axis_size("section"), lax.axis_size("expert")
+    rows, width = tokens.shape
+    exp_local, features, hidden = w_gate.shape
+    half = exp_local // HALVES
+    pad, scratch = sizes(n_sec, n_exp, tokens, w_gate, exp_local * n_exp)
+    used = 0
+    for shape, kind in scratch:
+        lead = 1
+        for extent in shape[:-2]:
+            lead *= extent
+        used += lead * (-(-shape[-2] // 16) * 16) * (-(-shape[-1] // 128) * 128) * jnp.dtype(kind).itemsize
+    used += 2 * n_sec * half * hidden * width + SPARE
+    depth = min(exp_local, (VMEM_BYTES - used) // (4 * features * hidden))
+    dma = pltpu.SemaphoreType.DMA
+    vmem, anyspace = pl.BlockSpec(memory_space=pltpu.VMEM), pl.BlockSpec(memory_space=pl.ANY)
+    return pl.pallas_call(
+        functools.partial(layer_kernel, n_sec, n_exp, depth),
+        out_shape=jax.ShapeDtypeStruct((rows, width), jnp.bfloat16),
+        in_specs=[vmem] * 4 + [anyspace] * 3,
+        out_specs=vmem,
+        scratch_shapes=[
+            pltpu.VMEM((depth, features, hidden), jnp.bfloat16),
+            pltpu.VMEM((depth, features, hidden), jnp.bfloat16),
+            pltpu.VMEM((n_sec, half, hidden, width), jnp.bfloat16),
+        ]
+        + [pltpu.VMEM(shape, kind) for shape, kind in scratch]
+        + [
+            dma((depth, 2)), dma((n_sec,)),
+            dma((n_sec,)), dma((n_sec,)),
+            dma((n_exp,)), dma((n_exp,)), dma((n_exp,)), dma((n_exp,)),
+            dma((n_exp,)), dma((n_exp,)),
+            dma((n_sec, n_exp)), dma((n_sec, n_exp)),
+            dma((n_sec - 1,)), dma((n_sec - 1,)),
+        ],
+        compiler_params=pltpu.CompilerParams(
+            collective_id=0, has_side_effects=True, vmem_limit_bytes=VMEM_BYTES
+        ),
+    )(tokens, scales, expert_ids, gate_fixed, w_gate, w_up, w_down)
+
+
+SPARE = 1 << 20
+
+
+def layer(tokens, scales, expert_ids, gate_fixed, w_gate, w_up, w_down):
+    n_exp = lax.axis_size("expert")
+    width = tokens.shape[1]
+    exp_local, _, hidden = w_gate.shape
+    fits = width % 128 == 0 and hidden % 128 == 0 and exp_local % HALVES == 0 and n_exp <= 16
+    body = fused if fits and n_exp % 2 == 0 else shards
+    return body(tokens, scales, expert_ids, gate_fixed, w_gate, w_up, w_down)
+
+
 def solution(mesh):
     placed = (
         P("expert", "section"),
@@ -69,5 +372,5 @@
         P("expert", "section", None),
     )
     return jax.shard_map(
-        shards, mesh=mesh, in_specs=placed, out_specs=P("expert", "section"), check_vma=False
+        layer, mesh=mesh, in_specs=placed, out_specs=P("expert", "section"), check_vma=False
     )

time: 200 us -> 49.4 us (0.25)
  local copies, waits for them, and re-layouts: 85.9 us -> 4.07 us
  Pallas kernels: 0 us -> 45.1 us
  blocking collectives: 32.9 us -> 0 us
  matrix products: 32.6 us -> 0 us
  waiting for transfers between devices: 29.3 us -> 0 us
  between operations: 13.5 us -> 0.01 us
  starting transfers between devices: 3.68 us -> 0 us
    unnamed x10 -> x3, local copies, waits for them, and re-layouts: 75.2 us -> 4.07 us
    pallas_call x0 -> x1, Pallas kernels: none -> 45.1 us  [fused(): pl.pallas_call(functools.partial(layer_kernel, n_sec, n_exp, depth), out_...]
    dot_general x4 -> x0, matrix products: 32.6 us -> none  [the longest x1 20.1 us: shards(): jnp.einsum('self,efd->seld', hidden, w_down, preferred_element_type=jnp.f...]
    unnamed x2 -> x0, waiting for transfers between devices: 23 us -> none
    all_gather x1 -> x0, blocking collectives: 21.3 us -> none  [shards(): lax.all_gather(lax.all_to_all(outgoing, 'expert', split_axis=0, concat_ax...]
    all_to_all x1 -> x0, blocking collectives: 11.5 us -> none  [shards(): lax.all_to_all(outgoing, 'expert', split_axis=0, concat_axis=0, tiled=True)]
    reduce_scatter x1 -> x0, local copies, waits for them, and re-layouts: 9.41 us -> none  [shards(): lax.psum_scatter(partial_rows.astype(jnp.float32).astype(jnp.bfloat16), '...]
    all_to_all x1 -> x0, waiting for transfers between devices: 6.36 us -> none  [shards(): lax.all_to_all(summed.astype(jnp.bfloat16), 'expert', split_axis=0, conca...]
  transfers between devices with their start and end apart: 2 -> 0, of which waited for: 2 -> 0; matrix products, arithmetic and copies ran while one was open for 0% -> 0% of each run, Pallas kernels for 0% -> 0%
where the time goes in v1:
time: 49.4 us; the launch traced here: 49.1 us
  Pallas kernels  45.1 us (91%)
  local copies, waits for them, and re-layouts  4.07 us (8%)
    pallas_call x1, Pallas kernels, fused(): pl.pallas_call(functools.partial(layer_kernel, n_sec, n_exp, depth), out_...  45.1 us
    unnamed x3, local copies, waits for them, and re-layouts  4.07 us

profile of v1, /device:TPU:0, one launch (start us, length us, event | category | flops | bytes accessed | tf_op | source)
XLA Modules:
  0.0 49.1 jit_solution(16802182060041691330)
XLA Ops:
  0.0 1.4 %copy.8.id_ref = s32[12,8]{1,0:T(8,128)} copy(s32[12,8]{0,1:T(8,128)} %param.9) | data formatting | bytes 768 | tf_op args[2]
  1.4 1.4 %copy.9.gf_ref = s32[12,8]{1,0:T(8,128)} copy(s32[12,8]{0,1:T(8,128)} %param.10) | data formatting | bytes 768 | tf_op args[3]
  2.7 45.1 %shard_map.73 = bf16[12,896]{1,0:T(8,128)(2,1)} custom-call(bf16[12,896]{1,0:T(8,128)(2,1)} %tok_ref.1, f32[12,28]{1,0:T(8,128)} %sc_ref.1, s32[12,8]{1,0:T(8,128)} %copy.8.id_ref, s32[12,8]{1,0:T(8,128)} %copy.9.gf_ref, bf16[8,3584,512]{2,1,0:T(8,128)(2,1)} %wg_ref.1, bf16[8,3584,512]{2,1,0:T(8,128)(2,1)} %wu_ref.1, bf16[8,512,3584]{2,1,0:T(8,128)(2,1)} %wd_ref.1), custom_call_target="tpu_custom_call" | custom-call | tf_op jit(solution)/shard_map/pallas_call | solution.py:327
  47.8 1.4 %copy.11 = bf16[12,896]{1,0:T(8,128)(2,1)} copy(bf16[12,896]{1,0:T(8,128)(2,1)} %shard_map.73) | data formatting | bytes 43008
